TPU v7x, 32 devices: a whole 2x2x4 slice. The times are simulated.
32 devices in a mesh: replica: 8 (over z, core), shard: 4 (over y, x).
Axes of the slice: x: 2, y: 2, z: 4, core: 2. Of those that a mesh axis runs over, the one named last changes fastest.
Arguments:
- hidden_in: bfloat16 [4, 2048, 2048], P('shard', 'replica'), may hold values from -6 to 6
- piece_index: int32 [4, 2048], P('shard', 'replica'), may hold values from -1 to 7, as said below
- pad_flags: int32 [4, 2048], P('shard', 'replica'), may hold values from 0 to 1, as said below
- cotangent: bfloat16 [4, 2048, 2048], P('shard', 'replica'), may hold values from -6 to 6
- query_weight: bfloat16 [2048, 2048], P('shard'), may hold values from -0.125 to 0.125
- key_weight: bfloat16 [2048, 2048], P('shard'), may hold values from -0.125 to 0.125
- value_weight: bfloat16 [2048, 2048], P('shard'), may hold values from -0.125 to 0.125
- output_weight: bfloat16 [2048, 2048], P('shard'), may hold values from -0.125 to 0.125
- gate_weight: bfloat16 [2048, 8192], P('shard'), may hold values from -0.125 to 0.125
- up_weight: bfloat16 [2048, 8192], P('shard'), may hold values from -0.125 to 0.125
- down_weight: bfloat16 [8192, 2048], P('shard'), may hold values from -0.0625 to 0.0625
- query_gain: bfloat16 [2048], P('shard'), may hold values from 0.25 to 1.75
- key_gain: bfloat16 [2048], P('shard'), may hold values from 0.25 to 1.75
- attention_gain: bfloat16 [2048], P('shard'), may hold values from 0.25 to 1.75
- feed_gain: bfloat16 [2048], P('shard'), may hold values from 0.25 to 1.75
Outputs:
- result: float32 [4, 2048, 2048], P('shard', 'replica')
- grad_hidden: float32 [4, 2048, 2048], P('shard', 'replica')
- grad_query_weight: float32 [2048, 2048], P('shard')
- grad_key_weight: float32 [2048, 2048], P('shard')
- grad_value_weight: float32 [2048, 2048], P('shard')
- grad_output_weight: float32 [2048, 2048], P('shard')
- grad_gate_weight: float32 [2048, 8192], P('shard')
- grad_up_weight: float32 [2048, 8192], P('shard')
- grad_down_weight: float32 [8192, 2048], P('shard')
- grad_query_gain: float32 [2048], P('shard')
- grad_key_gain: float32 [2048], P('shard')
- grad_attention_gain: float32 [2048], P('shard')
- grad_feed_gain: float32 [2048], P('shard')
- stats: float32 [3], replicated
Inputs may be any that keep to these rules, and one draw needn't show every extreme that they name: `piece_index`: -1 marks text. A picture piece is an aligned run of 256 tokens of one sequence, all holding that run's index within the sequence; the first run of every sequence is text and the last run of every sequence is a picture piece. `pad_flags`: each sequence ends in a run of one or more padded tokens and has none elsewhere.
All inputs are finite; a program needn't handle non-finite values.
Results may differ from a plain program's by a relative error of at most 0.025.
Values may be sent and summed in bfloat16 or wider, within the bound.
No kernel may reach another device: no remote copies, remote signals or barrier semaphores. Data moves between devices by JAX's collectives and lax.ppermute only.
A program may use at most 576 MiB of HBM per device.

v0:
```python
import math
import jax
import jax.numpy as jnp
from jax import lax
from jax.sharding import PartitionSpec as P

HEADS = 16
HEAD = 128
epsilon = 1e-06
theta_base = 500000.0
masked_score = -1e30


def norm_rows(values, gain):
    scaled = values * lax.rsqrt(jnp.mean(values * values, axis=-1, keepdims=True) + epsilon)
    return scaled * gain


def angle_table(positions):
    half_head = HEAD // 2
    rates = theta_base ** (-jnp.arange(half_head).astype(jnp.float32) * (2.0 / HEAD))
    angles = positions.astype(jnp.float32)[:, None] * rates[None, :]
    return (jnp.cos(angles), jnp.sin(angles))


def rotate(values, cosine, sine):
    half_head = HEAD // 2
    first_half = values[..., :half_head]
    second_half = values[..., half_head:]
    cos_wide = cosine[:, None, :]
    sin_wide = sine[:, None, :]
    return jnp.concatenate(
        [
            first_half * cos_wide - second_half * sin_wide,
            second_half * cos_wide + first_half * sin_wide,
        ],
        axis=-1,
    )


def turn_heads(flat_rows, gain, cosine, sine):
    rows_here = flat_rows.shape[0]
    normed = norm_rows(flat_rows, gain).reshape(rows_here, HEADS, HEAD)
    return rotate(normed, cosine, sine).reshape(rows_here, HEADS * HEAD)


def contract_rows(left, right):
    return lax.dot_general(
        left, right, (((0,), (0,)), ((), ())), preferred_element_type=jnp.float32
    )


def contract_cols(left, right):
    return lax.dot_general(
        left, right, (((1,), (1,)), ((), ())), preferred_element_type=jnp.float32
    )


def block_scores(queries, keys_part, info_part, query_place, query_piece, start_key):
    rows_here = queries.shape[0]
    block_rows = keys_part.shape[0]
    scores = jnp.einsum(
        "qhd,khd->hqk",
        queries.reshape(rows_here, HEADS, HEAD),
        keys_part.reshape(block_rows, HEADS, HEAD),
        preferred_element_type=jnp.float32,
    ) * HEAD ** (-0.5)
    key_place = start_key + jnp.arange(block_rows, dtype=jnp.int32)
    key_piece = info_part.astype(jnp.float32)
    allowed = (key_place[None, :] <= query_place[:, None]) | (query_piece[:, None] >= 0.0) & (
        query_piece[:, None] == key_piece[None, :]
    )
    allowed = allowed & (key_piece[None, :] > -1.5)
    return jnp.where(allowed[None], scores, masked_score)


def per_device(
    hidden_in,
    piece_index,
    pad_flags,
    cotangent,
    query_weight,
    key_weight,
    value_weight,
    output_weight,
    gate_weight,
    up_weight,
    down_weight,
    query_gain,
    key_gain,
    attention_gain,
    feed_gain,
):
    tokens = hidden_in[0]
    rows_here = tokens.shape[0]
    width_all = tokens.shape[1]
    hidden_all = gate_weight.shape[1]
    seq_len = rows_here * lax.axis_size("replica")
    first_row = lax.axis_index("replica") * rows_here
    positions = first_row + jnp.arange(rows_here, dtype=jnp.int32)
    cosine, sine = angle_table(positions)
    score_scale = HEAD ** (-0.5)
    input_whole = ()
    feed_whole = ()
    start = jnp.int32(0)
    whole_in = input_whole
    piece_query = lax.all_gather(query_weight, "shard", axis=0, tiled=True)
    piece_key = lax.all_gather(key_weight, "shard", axis=0, tiled=True)
    piece_value = lax.all_gather(value_weight, "shard", axis=0, tiled=True)
    piece_out = lax.all_gather(output_weight, "shard", axis=0, tiled=True)
    gain_one = lax.all_gather(query_gain, "shard", axis=0, tiled=True)
    gain_two = lax.all_gather(key_gain, "shard", axis=0, tiled=True)
    gain_three = lax.all_gather(attention_gain, "shard", axis=0, tiled=True)
    gain_four = lax.all_gather(feed_gain, "shard", axis=0, tiled=True)
    columns = tokens
    sums = tuple(
        (
            jnp.dot(columns, piece, preferred_element_type=jnp.float32)
            for piece in (piece_query, piece_key, piece_value)
        )
    )
    stacked = jnp.stack([gain_one, gain_two, gain_three, gain_four])
    gain_rows = stacked
    whole_in = tuple(
        (
            lax.dynamic_update_slice_in_dim(whole, piece, start, 0)
            for whole, piece in zip(whole_in, (piece_query, piece_key, piece_value))
        )
    )
    (query_raw, key_raw, value_raw), out_whole, gain_rows, input_whole = (
        sums,
        piece_out,
        gain_rows,
        whole_in,
    )
    gains_wide = gain_rows.astype(jnp.float32)

    def turn_local(raw_rows, gain):
        return turn_heads(raw_rows, gain, cosine, sine)

    query_turned, query_pull = jax.vjp(turn_local, query_raw, gains_wide[0])
    key_turned, key_pull = jax.vjp(turn_local, key_raw, gains_wide[1])
    query_low = query_turned.astype(jnp.bfloat16)
    key_low = key_turned.astype(jnp.bfloat16)
    value_low = value_raw.astype(jnp.bfloat16)
    key_info = jnp.where(pad_flags[0] > 0, -2, piece_index[0]).astype(jnp.bfloat16)
    keys_all, values_all, info_all = (
        lax.all_gather(key_low, "replica", axis=0, tiled=True),
        lax.all_gather(value_low, "replica", axis=0, tiled=True),
        lax.all_gather(key_info, "replica", axis=0, tiled=True),
    )
    query_piece = piece_index[0].astype(jnp.float32)
    block_rows = math.gcd(seq_len, 512)
    block_count = seq_len // block_rows

    def scores_at(index):
        start_key = index * block_rows
        keys_part = lax.dynamic_slice_in_dim(keys_all, start_key, block_rows, 0)
        info_part = lax.dynamic_slice_in_dim(info_all, start_key, block_rows, 0)
        return block_scores(query_low, keys_part, info_part, positions, query_piece, start_key)

    def bound_step(index, carried):
        highest, summed = carried
        scores = scores_at(index)
        raised = jnp.maximum(highest, jnp.max(scores, axis=-1))
        summed = summed * jnp.exp(highest - raised) + jnp.sum(
            jnp.exp(scores - raised[..., None]), axis=-1
        )
        return (raised, summed)

    highest, summed = lax.fori_loop(
        0,
        block_count,
        bound_step,
        (
            jnp.full((HEADS, rows_here), masked_score, jnp.float32),
            jnp.zeros((HEADS, rows_here), jnp.float32),
        ),
    )
    log_total = highest + jnp.log(summed)

    def value_step(index, carried):
        start_key = index * block_rows
        weights_low = jnp.exp(scores_at(index) - log_total[..., None]).astype(jnp.bfloat16)
        values_part = lax.dynamic_slice_in_dim(values_all, start_key, block_rows, 0).reshape(
            block_rows, HEADS, HEAD
        )
        return carried + jnp.einsum(
            "hqk,khd->qhd", weights_low, values_part, preferred_element_type=jnp.float32
        )

    mixed = lax.fori_loop(
        0, block_count, value_step, jnp.zeros((rows_here, HEADS, HEAD), jnp.float32)
    )
    attended_low = mixed.reshape(rows_here, width_all).astype(jnp.bfloat16)
    branch_attn = jnp.dot(attended_low, out_whole, preferred_element_type=jnp.float32)
    normed_attn, attn_pull = jax.vjp(norm_rows, branch_attn, gains_wide[2])
    residual = tokens.astype(jnp.float32) + normed_attn
    residual_low = residual.astype(jnp.bfloat16)
    pieces = (
        lax.all_gather(gate_weight, "shard", axis=0, tiled=True),
        lax.all_gather(up_weight, "shard", axis=0, tiled=True),
    )
    start = jnp.int32(0)
    whole_list = feed_whole
    columns = residual_low
    sums = tuple((jnp.dot(columns, piece, preferred_element_type=jnp.float32) for piece in pieces))
    whole_list = tuple(
        (
            lax.dynamic_update_slice_in_dim(whole, piece, start, 0)
            for whole, piece in zip(whole_list, pieces)
        )
    )
    (gate_sum, up_sum), feed_whole = (sums, whole_list)

    def activate(gate_values, up_values):
        return jax.nn.silu(gate_values) * up_values

    activated, act_pull = jax.vjp(activate, gate_sum, up_sum)
    activated_low = activated.astype(jnp.bfloat16)
    piece = lax.all_gather(down_weight, "shard", axis=0, tiled=True)
    columns = activated_low
    partial_sum = jnp.dot(columns, piece, preferred_element_type=jnp.float32)
    normed_feed, feed_pull = jax.vjp(norm_rows, partial_sum, gains_wide[3])
    result = residual + normed_feed
    grad_out = cotangent[0].astype(jnp.float32)
    grad_feed, grad_feed_gain = feed_pull(grad_out)
    grad_feed_low = grad_feed.astype(jnp.bfloat16)
    grad_act = contract_cols(
        grad_feed_low, lax.all_gather(down_weight, "shard", axis=0, tiled=True)
    )
    down_share = lax.psum_scatter(
        contract_rows(activated_low, grad_feed_low).astype(jnp.bfloat16),
        "shard",
        scatter_dimension=0,
        tiled=True,
    ).astype(jnp.float32)
    grad_gate, grad_up = act_pull(grad_act)
    grad_gate_low = grad_gate.astype(jnp.bfloat16)
    grad_up_low = grad_up.astype(jnp.bfloat16)
    pieces = (
        lax.all_gather(gate_weight, "shard", axis=0, tiled=True),
        lax.all_gather(up_weight, "shard", axis=0, tiled=True),
    )
    part_sum = contract_cols(grad_gate_low, pieces[0]) + contract_cols(grad_up_low, pieces[1])
    grad_feed_in = part_sum
    grad_both = jnp.concatenate([grad_gate_low, grad_up_low], axis=1)
    feed_share = lax.psum_scatter(
        contract_rows(residual_low, grad_both).astype(jnp.bfloat16),
        "shard",
        scatter_dimension=0,
        tiled=True,
    ).astype(jnp.float32)
    grad_resid = grad_out + grad_feed_in
    grad_branch, grad_attention_gain = attn_pull(grad_resid)
    grad_branch_low = grad_branch.astype(jnp.bfloat16)
    grad_attended = contract_cols(
        grad_branch_low, lax.all_gather(output_weight, "shard", axis=0, tiled=True)
    )
    grad_mixed = grad_attended.astype(jnp.bfloat16).reshape(rows_here, HEADS, HEAD)
    delta = jnp.einsum("qhd,qhd->hq", grad_mixed.astype(jnp.float32), mixed)
    query_heads = query_low.reshape(rows_here, HEADS, HEAD)

    def back_step(index, carried):
        grad_query, grad_keys, grad_values = carried
        start_key = index * block_rows
        probs = jnp.exp(scores_at(index) - log_total[..., None])
        keys_part = lax.dynamic_slice_in_dim(keys_all, start_key, block_rows, 0).reshape(
            block_rows, HEADS, HEAD
        )
        values_part = lax.dynamic_slice_in_dim(values_all, start_key, block_rows, 0).reshape(
            block_rows, HEADS, HEAD
        )
        value_share = jnp.einsum(
            "hqk,qhd->khd",
            probs.astype(jnp.bfloat16),
            grad_mixed,
            preferred_element_type=jnp.float32,
        )
        grad_probs = jnp.einsum(
            "qhd,khd->hqk", grad_mixed, values_part, preferred_element_type=jnp.float32
        )
        grad_scores = (probs * (grad_probs - delta[..., None])).astype(jnp.bfloat16)
        grad_query = grad_query + jnp.einsum(
            "hqk,khd->qhd", grad_scores, keys_part, preferred_element_type=jnp.float32
        )
        key_share = (
            jnp.einsum("hqk,qhd->khd", grad_scores, query_heads, preferred_element_type=jnp.float32)
            * score_scale
        )
        grad_keys = lax.dynamic_update_slice_in_dim(
            grad_keys, key_share.reshape(block_rows, width_all), start_key, 0
        )
        grad_values = lax.dynamic_update_slice_in_dim(
            grad_values, value_share.reshape(block_rows, width_all), start_key, 0
        )
        return (grad_query, grad_keys, grad_values)

    zero_keys = jnp.zeros((seq_len, width_all), jnp.float32)
    grad_query, grad_keys, grad_values = lax.fori_loop(
        0,
        block_count,
        back_step,
        (jnp.zeros((rows_here, HEADS, HEAD), jnp.float32), zero_keys, zero_keys),
    )
    key_sum, value_sum = (
        lax.psum_scatter(
            grad_keys.astype(jnp.bfloat16), "replica", scatter_dimension=0, tiled=True
        ).astype(jnp.float32),
        lax.psum_scatter(
            grad_values.astype(jnp.bfloat16), "replica", scatter_dimension=0, tiled=True
        ).astype(jnp.float32),
    )
    grad_query_raw, grad_query_gain = query_pull(
        (grad_query * score_scale).reshape(rows_here, width_all)
    )
    grad_key_raw, grad_key_gain = key_pull(key_sum)
    query_back_low = grad_query_raw.astype(jnp.bfloat16)
    key_back_low = grad_key_raw.astype(jnp.bfloat16)
    value_back_low = value_sum.astype(jnp.bfloat16)
    pieces = (
        lax.all_gather(query_weight, "shard", axis=0, tiled=True),
        lax.all_gather(key_weight, "shard", axis=0, tiled=True),
        lax.all_gather(value_weight, "shard", axis=0, tiled=True),
    )
    part_sum = (
        contract_cols(query_back_low, pieces[0])
        + contract_cols(key_back_low, pieces[1])
        + contract_cols(value_back_low, pieces[2])
    )
    grad_tokens = grad_resid + part_sum
    grad_inputs = jnp.concatenate([query_back_low, key_back_low, value_back_low], axis=1)
    input_share = lax.psum_scatter(
        jnp.concatenate(
            [contract_rows(tokens, grad_inputs), contract_rows(attended_low, grad_branch_low)],
            axis=1,
        ).astype(jnp.bfloat16),
        "shard",
        scatter_dimension=0,
        tiled=True,
    ).astype(jnp.float32)
    input_share, feed_share, down_share = (
        lax.psum(input_share.astype(jnp.bfloat16), "replica").astype(jnp.float32),
        lax.psum(feed_share.astype(jnp.bfloat16), "replica").astype(jnp.float32),
        lax.psum(down_share.astype(jnp.bfloat16), "replica").astype(jnp.float32),
    )
    valid = (pad_flags[0] == 0).astype(jnp.float32)[:, None]
    stat_terms = jnp.stack(
        [
            jnp.sum(valid * result * result),
            jnp.sum(valid * branch_attn * branch_attn),
            jnp.sum(valid * partial_sum * partial_sum),
            jnp.sum(valid),
        ]
    )
    gain_terms = jnp.stack([grad_query_gain, grad_key_gain, grad_attention_gain, grad_feed_gain])
    gain_terms, stat_terms = lax.psum((gain_terms, stat_terms), ("replica", "shard"))
    gain_width = query_gain.shape[0]
    gain_mine = lax.dynamic_slice_in_dim(
        gain_terms, lax.axis_index("shard") * gain_width, gain_width, 1
    )
    stats = jnp.sqrt(stat_terms[:3] / (stat_terms[3] * width_all))
    return (
        result[None],
        grad_tokens[None],
        input_share[:, :width_all],
        input_share[:, width_all : 2 * width_all],
        input_share[:, 2 * width_all : 3 * width_all],
        input_share[:, 3 * width_all :],
        feed_share[:, :hidden_all],
        feed_share[:, hidden_all:],
        down_share,
        gain_mine[0],
        gain_mine[1],
        gain_mine[2],
        gain_mine[3],
        stats,
    )


def solution(mesh):
    placed = (
        P("shard", "replica", None),
        P("shard", "replica"),
        P("shard", "replica"),
        P("shard", "replica", None),
        P("shard", None),
        P("shard", None),
        P("shard", None),
        P("shard", None),
        P("shard", None),
        P("shard", None),
        P("shard", None),
        P("shard"),
        P("shard"),
        P("shard"),
        P("shard"),
    )
    return jax.shard_map(
        per_device,
        mesh=mesh,
        in_specs=placed,
        out_specs=(
            P("shard", "replica", None),
            P("shard", "replica", None),
            P("shard", None),
            P("shard", None),
            P("shard", None),
            P("shard", None),
            P("shard", None),
            P("shard", None),
            P("shard", None),
            P("shard"),
            P("shard"),
            P("shard"),
            P("shard"),
            P(),
        ),
        check_vma=False,
    )
```

profile of v0, /device:TPU:0, one launch (start us, length us, event | category | flops | bytes accessed | tf_op | source)
XLA Modules:
  0.0 3683.2 jit_solution(10131605898892978450)
XLA Ops:
  9.5 90.7 %all-gather.15.cloned.1.call-done = bf16[2048,2048]{1,0:T(8,128)(2,1)} async-done(((bf16[512,2048]{1,0:T(8,128)(2,1)}), bf16[2048,2048]{1,0:T(8,128)(2,1)}) %all-gather.15.cloned.1.call-update) | async-done | bytes 8388624 | tf_op jit(solution)/shard_map/all_gather | solution.py:109
  100.2 6.7 convolution_convert_fusion.4
  107.1 8.0 all-gather.1
  115.1 7.1 all-gather.2
  122.2 8.0 all-gather.3
  130.2 7.1 all-gather.4
  138.4 51.5 %all-gather.19.cloned.1.call-done = bf16[2048,2048]{1,0:T(8,128)(2,1)} async-done(((bf16[512,2048]{1,0:T(8,128)(2,1)}), bf16[2048,2048]{1,0:T(8,128)(2,1)}) %all-gather.19.cloned.1.call-update) | async-done | bytes 8388624 | tf_op jit(solution)/shard_map/all_gather | solution.py:108
  189.9 5.8 multiply_reduce_fusion.10
  205.4 11.7 all-gather
  217.7 61.7 %all-gather.23.cloned.1.call-done = bf16[2048,2048]{1,0:T(8,128)(2,1)} async-done(((bf16[512,2048]{1,0:T(8,128)(2,1)}), bf16[2048,2048]{1,0:T(8,128)(2,1)}) %all-gather.23.cloned.1.call-update) | async-done | bytes 8388624 | tf_op jit(solution)/shard_map/all_gather | solution.py:107
  279.4 5.8 multiply_reduce_fusion.9
  291.6 71.9 %all-gather.17.cloned.1.call-done = bf16[2048,2048]{1,0:T(8,128)(2,1)} async-done(((bf16[256,2048]{1,0:T(8,128)(2,1)}), bf16[2048,2048]{1,0:T(8,128)(2,1)}) %all-gather.17.cloned.1.call-update) | async-done | bytes 8388624 | tf_op jit(solution)/shard_map/all_gather | solution.py:149
  363.5 12.3 copy.126
  375.9 70.7 %all-gather.21.cloned.1.call-done = bf16[2048,2048]{0,1:T(8,128)(2,1)} async-done(((bf16[256,2048]{0,1:T(8,128)(2,1)}), bf16[2048,2048]{0,1:T(8,128)(2,1)}) %all-gather.21.cloned.1.call-update) | async-done | bytes 8388624 | tf_op jit(solution)/shard_map/all_gather | solution.py:148
  446.6 51.6 %while.48 = (s32[]{:T(128)}, f32[16,256]{1,0:T(8,128)S(1)}, f32[16,256]{1,0:T(8,128)S(1)}, f32[256]{0:T(256)S(1)}, bf16[2048]{0:T(1024)(128)(2,1)S(1)}, /*index=...) while((s32[]{:T(128)}, f32[16,256]{1,0:T(8,128)S(1)}, ...), condition=%wide.region_5.6_spmd.clone, body=%wide.region_2.5_spmd.clone.sunk | while | flops 552229376 | bytes 24739520 | solution.py:171
  454.1 6.3 exponential_reduce_fusion.2
  498.2 42.5 %while.49 = (s32[]{:T(128)}, f32[256,16,128]{0,2,1:T(8,128)}, bf16[2048,2048]{0,1:T(8,128)(2,1)}, f32[256]{0:T(256)S(1)}, bf16[2048]{0:T(1024)(128)(2,1)S(1)}, /...) while((s32[]{:T(128)}, f32[256,16,128]{0,2,1:T(8,128)}, ...), condition=%wide.region_7.8_spmd.clone, body=%wide.region_6.7_spmd.clone.sunk | while | flops 1083836928 | bytes 18120392 | solution.py:192
  502.5 5.9 bitcast_add_fusion.4
  512.7 6.5 bitcast_add_fusion.4
  523.4 6.5 bitcast_add_fusion.4
  534.2 6.5 bitcast_add_fusion.4
  543.2 9.1 multiply_reduce_fusion.8
  554.1 279.1 %all-gather.27.cloned.1.call-done = bf16[2048,8192]{1,0:T(8,128)(2,1)} async-done(((bf16[512,8192]{1,0:T(8,128)(2,1)}), bf16[2048,8192]{1,0:T(8,128)(2,1)}) %all-gather.27.cloned.1.call-update) | async-done | bytes 33554448 | tf_op jit(solution)/shard_map/all_gather | solution.py:201
  833.2 22.2 fusion.92
  855.5 276.8 %all-gather.29.cloned.1.call-done = bf16[2048,8192]{1,0:T(8,128)(2,1)} async-done(((bf16[512,8192]{1,0:T(8,128)(2,1)}), bf16[2048,8192]{1,0:T(8,128)(2,1)}) %all-gather.29.cloned.1.call-update) | async-done | bytes 33554448 | tf_op jit(solution)/shard_map/all_gather | solution.py:202
  1132.3 26.9 multiply_convert_fusion.1
  1159.2 272.2 %all-gather.31.cloned.1.call-done = bf16[8192,2048]{1,0:T(8,128)(2,1)} async-done(((bf16[2048,2048]{1,0:T(8,128)(2,1)}), bf16[8192,2048]{1,0:T(8,128)(2,1)}) %all-gather.31.cloned.1.call-update) | async-done | bytes 33554448 | tf_op jit(solution)/shard_map/all_gather | solution.py:221
  1431.4 16.6 multiply_reduce_fusion.7
  1450.1 22.0 multiply_convert_fusion
  1472.1 17.1 fusion.93
  1489.2 20.5 multiply_reduce_fusion.1
  1531.4 106.4 %while.50 = (s32[]{:T(128)}, f32[256,16,128]{0,2,1:T(8,128)}, bf16[2048,2048]{0,1:T(8,128)(2,1)}, bf16[2048,2048]{1,0:T(8,128)(2,1)}, bf16[2048,2048]{0,1:T(8,12...) while((s32[]{:T(128)}, f32[256,16,128]{0,2,1:T(8,128)}, ...), condition=%wide.region_13.14_spmd.clone, body=%wide.region_12.13_spmd.clone.sunk | while | flops 2709129728 | bytes 103219016 | solution.py:300
  1639.7 16.4 convolution_convert_fusion.1
  1665.9 61.8 %reduce-scatter.10.cloned.1.call-done = bf16[256,2048]{0,1:T(8,128)(2,1)} async-done(((bf16[2048,2048]{0,1:T(8,128)(2,1)}), bf16[256,2048]{0,1:T(8,128)(2,1)}) %reduce-scatter.10.cloned.1.call-update) | async-done | bytes 1048592 | tf_op jit(solution)/shard_map/reduce_scatter | solution.py:307
  1741.6 76.9 %reduce-scatter.12.cloned.1.call-done = bf16[256,2048]{1,0:T(8,128)(2,1)} async-done(((bf16[2048,2048]{1,0:T(8,128)(2,1)}), bf16[256,2048]{1,0:T(8,128)(2,1)}) %reduce-scatter.12.cloned.1.call-update) | async-done | bytes 1048592 | tf_op jit(solution)/shard_map/reduce_scatter | solution.py:310
  1818.5 13.4 convert_bitcast_fusion
  1831.8 24.4 pad_maximum_fusion
  1857.4 29.1 convolution_convert_fusion
  1886.8 221.6 %reduce-scatter.18.cloned.1.call-done = bf16[2048,2048]{1,0:T(8,128)(2,1)} async-done(((bf16[8192,2048]{1,0:T(8,128)(2,1)}), bf16[2048,2048]{1,0:T(8,128)(2,1)}) %reduce-scatter.18.cloned.1.call-update) | async-done | bytes 8388624
  2108.4 292.0 %reduce-scatter.14.cloned.1.call-done = bf16[512,8192]{0,1:T(8,128)(2,1)} async-done(((bf16[2048,8192]{0,1:T(8,128)(2,1)}), bf16[512,8192]{0,1:T(8,128)(2,1)}) %reduce-scatter.14.cloned.1.call-update) | async-done | bytes 8388624 | tf_op jit(solution)/shard_map/reduce_scatter | solution.py:333
  2400.5 561.2 %reduce-scatter.16.cloned.1.call-done = bf16[512,16384]{1,0:T(8,128)(2,1)} async-done(((bf16[2048,16384]{1,0:T(8,128)(2,1)}), bf16[512,16384]{1,0:T(8,128)(2,1)}) %reduce-scatter.16.cloned.1.call-update) | async-done | bytes 16777232
  2965.6 41.1 %all-reduce.6 = (f32[4,2048]{1,0:T(4,128)S(1)}, f32[4]{0:T(128)S(1)}) all-reduce(f32[4,2048]{1,0:T(4,128)S(1)} %pad_maximum_fusion.2, f32[4]{0:T(128)S(1)} %pad_maximum_fusion.3), channel_id=1, replica_groups=mesh['replica'=8,'shard'=4] {'replica','shard'}, use_global_device_ids=true, to_apply=%region_28.29 | all-reduce | flops 8196 | bytes 65568 | tf_op jit(solution)/shard_map/psum | solution.py:357
  3009.2 5.9 fusion.94
  3015.1 6.1 convolution_add_fusion.2
  3025.0 591.2 %all-reduce.10.cloned.1.call-done = (bf16[512,8192]{0,1:T(8,128)(2,1)}, bf16[512,16384]{1,0:T(8,128)(2,1)}, bf16[2048,2048]{1,0:T(8,128)(2,1)}) async-done(((bf16[512,8192]{0,1:T(8,128)(2,1)}, bf16[512,16384]{1,0:T(8,128)(2,1)}, bf16[2048,2048]{1,0:T(8,128)(2,1)}), (bf16[512,8192]{0,1:T(8,128)(2,1)}, bf16[512,16384]{1,0:T(8,128)(2,1)}, bf16[2048,2048]{1,0:T(8,128)(2,1)})) %all-reduce.10.cloned.1.call-update) | async-done | bytes 33554448 | tf_op jit(solution)/shard_map/psum | solution.py:343
  3616.1 16.9 fusion.86
  3633.0 10.4 fusion.87
  3664.8 11.7 convert_element_type.207
  (396 shorter events, 273.2 us)
Async XLA Ops:
  7.2 93.0 %all-gather.15.cloned.1.call-start = ((), (), s32[]{:S(2)}) async-start(), calls=%async_computation.5 | async-start | bytes 10485760 | tf_op jit(solution)/shard_map/all_gather | solution.py:109
  7.9 92.3 %copy-start.22 = (bf16[1,256,2048]{2,1,0:T(8,128)(2,1)S(1)}, bf16[1,256,2048]{2,1,0:T(8,128)(2,1)}, u32[]{:S(2)}) copy-start(bf16[1,256,2048]{2,1,0:T(8,128)(2,1)} %param.21) | copy-start | bytes 3145732
  7.9 181.9 %all-gather.19.cloned.1.call-start = ((), (), s32[]{:S(2)}) async-start(), calls=%async_computation.7 | async-start | bytes 10485760 | tf_op jit(solution)/shard_map/all_gather | solution.py:108
  8.7 270.7 %all-gather.23.cloned.1.call-start = ((), (), s32[]{:S(2)}) async-start(), calls=%async_computation.9 | async-start | bytes 10485760 | tf_op jit(solution)/shard_map/all_gather | solution.py:107
  9.4 97.6 %copy-start.62 = (bf16[512]{0:T(512)(128)(2,1)S(1)}, bf16[512]{0:T(512)(128)(2,1)}, u32[]{:S(2)}) copy-start(bf16[512]{0:T(512)(128)(2,1)} %param.32) | copy-start | bytes 3076
  9.4 97.6 %copy-start.63 = (bf16[512]{0:T(512)(128)(2,1)S(1)}, bf16[512]{0:T(512)(128)(2,1)}, u32[]{:S(2)}) copy-start(bf16[512]{0:T(512)(128)(2,1)} %param.33) | copy-start | bytes 3076
  9.4 97.6 %copy-start.64 = (bf16[512]{0:T(512)(128)(2,1)S(1)}, bf16[512]{0:T(512)(128)(2,1)}, u32[]{:S(2)}) copy-start(bf16[512]{0:T(512)(128)(2,1)} %param.34) | copy-start | bytes 3076
  9.4 97.6 %copy-start.65 = (bf16[512]{0:T(512)(128)(2,1)S(1)}, bf16[512]{0:T(512)(128)(2,1)}, u32[]{:S(2)}) copy-start(bf16[512]{0:T(512)(128)(2,1)} %param.35) | copy-start | bytes 3076
  9.4 354.1 %all-gather.17.cloned.1.call-start = ((), (), s32[]{:S(2)}) async-start(), calls=%async_computation.6 | async-start | bytes 9437184 | tf_op jit(solution)/shard_map/all_gather | solution.py:149
  106.9 339.7 %all-gather.21.cloned.1.call-start = ((), (), s32[]{:S(2)}) async-start(), calls=%async_computation.8 | async-start | bytes 9437184 | tf_op jit(solution)/shard_map/all_gather | solution.py:148
  137.7 151.1 %copy-start.30 = (f32[256,64]{0,1:T(8,128)}, f32[256,64]{0,1:T(8,128)S(1)}, u32[]{:S(2)}) copy-start(f32[256,64]{0,1:T(8,128)S(1)} %get-tuple-element.949) | copy-start | bytes 196612
  137.7 151.1 %copy-start.32 = (f32[256,64]{0,1:T(8,128)}, f32[256,64]{0,1:T(8,128)S(1)}, u32[]{:S(2)}) copy-start(f32[256,64]{0,1:T(8,128)S(1)} %get-tuple-element.950) | copy-start | bytes 196612
  138.4 57.3 %copy-start.42 = (f32[1,2048]{1,0:T(1,128)}, f32[1,2048]{1,0:T(1,128)S(1)}, u32[]{:S(2)}) copy-start(f32[1,2048]{1,0:T(1,128)S(1)} %get-tuple-element.948) | copy-start | bytes 24580
  138.4 147.4 %copy-start.40 = (f32[1,2048]{1,0:T(1,128)}, f32[1,2048]{1,0:T(1,128)S(1)}, u32[]{:S(2)}) copy-start(f32[1,2048]{1,0:T(1,128)S(1)} %get-tuple-element.947) | copy-start | bytes 24580
  202.4 340.7 %all-gather.25.cloned.1.call-start = ((), (), s32[]{:S(2)}) async-start(), calls=%async_computation.10 | async-start | bytes 10485760 | tf_op jit(solution)/shard_map/all_gather | solution.py:110
  203.0 630.2 %all-gather.27.cloned.1.call-start = ((), (), s32[]{:S(2)}) async-start(), calls=%async_computation.11 | async-start | bytes 41943040 | tf_op jit(solution)/shard_map/all_gather | solution.py:201
  203.8 928.5 %all-gather.29.cloned.1.call-start = ((), (), s32[]{:S(2)}) async-start(), calls=%async_computation.12 | async-start | bytes 41943040 | tf_op jit(solution)/shard_map/all_gather | solution.py:202
  204.5 1226.8 %all-gather.31.cloned.1.call-start = ((), (), s32[]{:S(2)}) async-start(), calls=%async_computation.13 | async-start | bytes 41943040 | tf_op jit(solution)/shard_map/all_gather | solution.py:221
  205.3 1522.3 %reduce-scatter.10.cloned.1.call-start = ((), (), s32[]{:S(2)}) async-start(), calls=%async_computation.14 | async-start | bytes 9437184 | tf_op jit(solution)/shard_map/reduce_scatter | solution.py:307
  291.0 84.9 %copy-start.4 = (bf16[256,16,128]{0,2,1:T(8,128)(2,1)}, bf16[256,16,128]{0,2,1:T(8,128)(2,1)S(1)}, u32[]{:S(2)}) copy-start(bf16[256,16,128]{0,2,1:T(8,128)(2,1)S(1)} %maximum_convert_fusion) | copy-start | bytes 3145732
  540.7 11.6 copy-start.1
  540.7 11.6 copy-start.36
  540.7 11.6 copy-start.38
  540.7 11.6 copy-start.46
  543.1 9.2 copy-start.14
  543.2 10.5 copy-start.23
  554.1 578.2 %copy-start.20 = (bf16[256,2048]{1,0:T(8,128)(2,1)}, bf16[256,2048]{1,0:T(8,128)(2,1)S(1)}, u32[]{:S(2)}) copy-start(bf16[256,2048]{1,0:T(8,128)(2,1)S(1)} %fusion.71) | copy-start | bytes 3145732
  1431.4 16.6 copy-start.27
  1431.4 16.6 copy-start.44
  1431.4 16.6 copy-start.55
  1448.0 24.1 copy-start.16
  1450.1 22.0 copy-start.53
  1472.1 39.6 %slice-start = ((s8[8388608]{0:T(1024)(128)(4,1)}), s8[4194304]{0:T(1024)(128)(4,1)S(1)}, s32[]{:S(2)}) async-start(s8[8388608]{0:T(1024)(128)(4,1)} %bitcast.255), calls=%async_computation.20 | async-start | bytes 8388608
  1489.2 20.5 copy-start.13
  1489.2 22.5 slice-start.1
  1637.8 180.7 %reduce-scatter.12.cloned.1.call-start = ((), (), s32[]{:S(2)}) async-start(), calls=%async_computation.15 | async-start | bytes 9437184 | tf_op jit(solution)/shard_map/reduce_scatter | solution.py:310
  1638.6 469.9 %reduce-scatter.18.cloned.1.call-start = ((), (), s32[]{:S(2)}) async-start(), calls=%async_computation.18 | async-start | bytes 41943040
  1656.2 744.3 %reduce-scatter.14.cloned.1.call-start = ((), (), s32[]{:S(2)}) async-start(), calls=%async_computation.16 | async-start | bytes 41943040 | tf_op jit(solution)/shard_map/reduce_scatter | solution.py:333
  1665.8 63.2 %copy-start.19 = (f32[256,16,128]{0,2,1:T(8,128)S(1)}, f32[256,16,128]{0,2,1:T(8,128)}, u32[]{:S(2)}) copy-start(f32[256,16,128]{0,2,1:T(8,128)} %broadcast_multiply_fusion) | copy-start | bytes 6291460
  1665.8 63.2 %copy-start.31 = (f32[256,64]{0,1:T(8,128)S(1)}, f32[256,64]{0,1:T(8,128)}, u32[]{:S(2)}) copy-start(f32[256,64]{0,1:T(8,128)} %copy-done.30) | copy-start | bytes 196612
  1665.8 63.2 %copy-start.33 = (f32[256,64]{0,1:T(8,128)S(1)}, f32[256,64]{0,1:T(8,128)}, u32[]{:S(2)}) copy-start(f32[256,64]{0,1:T(8,128)} %copy-done.32) | copy-start | bytes 196612
  1741.1 77.4 %copy-start.24 = (bf16[1,256,2048]{2,1,0:T(8,128)(2,1)S(1)}, bf16[1,256,2048]{2,1,0:T(8,128)(2,1)}, u32[]{:S(2)}) copy-start(bf16[1,256,2048]{2,1,0:T(8,128)(2,1)} %param.21) | copy-start | bytes 3145732
  1856.3 1105.4 %reduce-scatter.16.cloned.1.call-start = ((), (), s32[]{:S(2)}) async-start(), calls=%async_computation.17 | async-start | bytes 83886080
  1886.5 1729.6 %all-reduce.10.cloned.1.call-start = ((), (), s32[]{:S(2)}) async-start(), calls=%async_computation.19 | async-start | bytes 67108864 | tf_op jit(solution)/shard_map/psum | solution.py:343
  3009.2 12.0 slice-start.2
  3015.1 6.1 copy-start.29
  3015.1 6.1 copy-start.34
  3015.1 6.1 slice-start.3
  (47 other events, 104.9 us)
Sparse Core Ops, SparseCore 0:
  9.9 90.2 all-gather.14
  102.0 87.7 all-gather.18
  191.7 87.6 all-gather.22
  281.4 82.0 all-gather.16
  365.5 81.0 all-gather.20
  448.3 85.7 all-gather.24
  536.0 297.2 all-gather.26
  835.1 297.2 all-gather.28
  1134.1 297.2 all-gather.30
  1638.0 89.6 reduce-scatter.9
  1730.5 87.9 reduce-scatter.11
  1821.4 286.9 reduce-scatter.17
  2111.8 288.6 reduce-scatter.13
  2403.4 558.2 reduce-scatter.15
  2964.4 651.7 all-reduce.9
where the time goes:
time: 3690 us; the launch traced here: 3680 us
  waiting for transfers between devices  2980 us (81%)
  matrix products  339 us (9%)
  local copies, waits for them, and re-layouts  166 us (4%)
  other arithmetic  92.9 us (3%)
  blocking collectives  83.1 us (2%)
    unnamed x17, waiting for transfers between devices  788 us
    psum x1, waiting for transfers between devices, per_device(): lax.psum(input_share.astype(jnp.bfloat16), 'replica').astype(jnp.float32)  591 us
    reduce_scatter x1, waiting for transfers between devices, per_device(): lax.psum_scatter(jnp.concatenate([contract_rows(tokens, grad_inputs), con...  292 us
    all_gather x1, waiting for transfers between devices, per_device(): lax.all_gather(gate_weight, 'shard', axis=0, tiled=True)  279 us
    all_gather x1, waiting for transfers between devices, per_device(): lax.all_gather(up_weight, 'shard', axis=0, tiled=True)  277 us
    all_gather x1, waiting for transfers between devices, per_device(): piece = lax.all_gather(down_weight, 'shard', axis=0, tiled=True)  272 us
    all_gather x1, waiting for transfers between devices, per_device(): piece_value = lax.all_gather(value_weight, 'shard', axis=0, tiled=True)  90.7 us
    dot_general x7, matrix products, contract_cols(): lax.dot_general(left, right, (((1,), (1,)), ((), ())), preferred_element_...  77.7 us
  transfers between devices with their start and end apart: 15, of which 14 were waited for; matrix products, arithmetic and copies ran while one was open for 9% of the time, Pallas kernels for 0%

commit v1 on v0

--- a/solution.py
+++ b/solution.py
@@ -105,8 +105,13 @@
     start = jnp.int32(0)
     whole_in = input_whole
     piece_query = lax.all_gather(query_weight, "shard", axis=0, tiled=True)
-    piece_key = lax.all_gather(key_weight, "shard", axis=0, tiled=True)
-    piece_value = lax.all_gather(value_weight, "shard", axis=0, tiled=True)
+    piece_key, piece_value = jnp.split(
+        lax.all_gather(
+            jnp.concatenate([key_weight, value_weight], axis=1), "shard", axis=0, tiled=True
+        ),
+        [key_weight.shape[1]],
+        axis=1,
+    )
     piece_out = lax.all_gather(output_weight, "shard", axis=0, tiled=True)
     gain_one = lax.all_gather(query_gain, "shard", axis=0, tiled=True)
     gain_two = lax.all_gather(key_gain, "shard", axis=0, tiled=True)

time: 3690 us -> 3830 us (1.038)
  waiting for transfers between devices: 2980 us -> 3160 us
  local copies, waits for them, and re-layouts: 166 us -> 124 us
    all_gather x2 -> x3, waiting for transfers between devices: 142 us -> 244 us  [the longest x1 126 us: per_device(): lax.all_gather(jnp.concatenate([key_weight, value_weight], axis=1), 'shar...]
    psum x1, waiting for transfers between devices: 591 us -> 645 us  [per_device(): lax.psum(input_share.astype(jnp.bfloat16), 'replica').astype(jnp.float32)]
    all_gather x1, waiting for transfers between devices: 0.02 us -> 41.7 us  [per_device(): piece_out = lax.all_gather(output_weight, 'shard', axis=0, tiled=True)]
    all_gather x1, waiting for transfers between devices: 71.9 us -> 32.1 us  [per_device(): lax.all_gather(value_low, 'replica', axis=0, tiled=True)]
    unnamed x17 -> x18, waiting for transfers between devices: 788 us -> 787 us
  transfers between devices with their start and end apart: 15 -> 16, of which waited for: 14 -> 16; matrix products, arithmetic and copies ran while one was open for 9% -> 8% of each run, Pallas kernels for 0% -> 0%
where the time goes in v1:
time: 3830 us; the launch traced here: 3820 us
  waiting for transfers between devices  3160 us (83%)
  matrix products  342 us (9%)
  local copies, waits for them, and re-layouts  124 us (3%)
  other arithmetic  91.9 us (2%)
  blocking collectives  84.4 us (2%)
    unnamed x18, waiting for transfers between devices  787 us
    psum x1, waiting for transfers between devices, per_device(): lax.psum(input_share.astype(jnp.bfloat16), 'replica').astype(jnp.float32)  645 us
    all_gather x1, waiting for transfers between devices, per_device(): lax.all_gather(gate_weight, 'shard', axis=0, tiled=True)  292 us
    reduce_scatter x1, waiting for transfers between devices, per_device(): lax.psum_scatter(jnp.concatenate([contract_rows(tokens, grad_inputs), con...  292 us
    all_gather x1, waiting for transfers between devices, per_device(): lax.all_gather(up_weight, 'shard', axis=0, tiled=True)  277 us
    all_gather x1, waiting for transfers between devices, per_device(): piece = lax.all_gather(down_weight, 'shard', axis=0, tiled=True)  272 us
    all_gather x1, waiting for transfers between devices, per_device(): lax.all_gather(jnp.concatenate([key_weight, value_weight], axis=1), 'shar...  126 us
    dot_general x7, matrix products, contract_cols(): lax.dot_general(left, right, (((1,), (1,)), ((), ())), preferred_element_...  86.8 us
  transfers between devices with their start and end apart: 16, of which 16 were waited for; matrix products, arithmetic and copies ran while one was open for 8% of the time, Pallas kernels for 0%

profile of v1, /device:TPU:0, one launch (start us, length us, event | category | flops | bytes accessed | tf_op | source)
XLA Modules:
  0.0 3820.3 jit_solution(17358808176151524597)
XLA Ops:
  12.9 9.5 all-gather.1
  22.4 8.0 all-gather.2
  30.5 7.1 all-gather.3
  37.6 8.1 all-gather.4
  46.7 125.8 %all-gather.16.cloned.1.call-done = bf16[2048,4096]{1,0:T(8,128)(2,1)} async-done(((bf16[512,4096]{1,0:T(8,128)(2,1)}), bf16[2048,4096]{1,0:T(8,128)(2,1)}) %all-gather.16.cloned.1.call-update) | async-done | bytes 16777232 | tf_op jit(solution)/shard_map/all_gather | solution.py:109
  172.4 6.1 multiply_reduce_fusion.8
  181.0 8.0 fusion.71
  191.8 11.8 all-gather
  204.2 57.7 %all-gather.22.cloned.1.call-done = bf16[2048,2048]{1,0:T(8,128)(2,1)} async-done(((bf16[512,2048]{1,0:T(8,128)(2,1)}), bf16[2048,2048]{1,0:T(8,128)(2,1)}) %all-gather.22.cloned.1.call-update) | async-done | bytes 8388624 | tf_op jit(solution)/shard_map/all_gather | solution.py:107
  261.9 7.0 multiply_reduce_fusion.7
  273.2 73.5 %all-gather.20.cloned.1.call-done = bf16[2048,2048]{0,1:T(8,128)(2,1)} async-done(((bf16[256,2048]{0,1:T(8,128)(2,1)}), bf16[2048,2048]{0,1:T(8,128)(2,1)}) %all-gather.20.cloned.1.call-update) | async-done | bytes 8388624 | tf_op jit(solution)/shard_map/all_gather | solution.py:153
  346.6 50.6 %while.48 = (s32[]{:T(128)}, f32[16,256]{1,0:T(8,128)S(1)}, f32[16,256]{1,0:T(8,128)S(1)}, f32[256]{0:T(256)S(1)}, bf16[2048]{0:T(1024)(128)(2,1)S(1)}, /*index=...) while((s32[]{:T(128)}, f32[16,256]{1,0:T(8,128)S(1)}, ...), condition=%wide.region_5.6_spmd.clone, body=%wide.region_2.5_spmd.clone.sunk | while | flops 552229376 | bytes 24739520 | solution.py:176
  397.3 32.1 all-gather.18.cloned.1.call-done
  429.4 42.7 %while.49 = (s32[]{:T(128)}, f32[256,16,128]{0,2,1:T(8,128)}, bf16[2048,2048]{0,1:T(8,128)(2,1)}, f32[256]{0:T(256)S(1)}, bf16[2048]{0:T(1024)(128)(2,1)S(1)}, /...) while((s32[]{:T(128)}, f32[256,16,128]{0,2,1:T(8,128)}, ...), condition=%wide.region_7.8_spmd.clone, body=%wide.region_6.7_spmd.clone.sunk | while | flops 1083836928 | bytes 18120392 | solution.py:197
  444.1 6.5 bitcast_add_fusion.4
  454.9 6.5 bitcast_add_fusion.4
  465.7 6.5 bitcast_add_fusion.4
  475.2 41.7 %all-gather.24.cloned.1.call-done = bf16[2048,2048]{1,0:T(8,128)(2,1)} async-done(((bf16[512,2048]{1,0:T(8,128)(2,1)}), bf16[2048,2048]{1,0:T(8,128)(2,1)}) %all-gather.24.cloned.1.call-update) | async-done | bytes 8388624 | tf_op jit(solution)/shard_map/all_gather | solution.py:115
  516.9 6.2 multiply_reduce_fusion.6
  523.6 292.2 %all-gather.26.cloned.1.call-done = bf16[2048,8192]{1,0:T(8,128)(2,1)} async-done(((bf16[512,8192]{1,0:T(8,128)(2,1)}), bf16[2048,8192]{1,0:T(8,128)(2,1)}) %all-gather.26.cloned.1.call-update) | async-done | bytes 33554448 | tf_op jit(solution)/shard_map/all_gather | solution.py:206
  815.9 22.2 fusion.106
  838.1 276.8 %all-gather.28.cloned.1.call-done = bf16[2048,8192]{1,0:T(8,128)(2,1)} async-done(((bf16[512,8192]{1,0:T(8,128)(2,1)}), bf16[2048,8192]{1,0:T(8,128)(2,1)}) %all-gather.28.cloned.1.call-update) | async-done | bytes 33554448 | tf_op jit(solution)/shard_map/all_gather | solution.py:207
  1114.9 26.9 multiply_convert_fusion.1
  1141.8 272.2 %all-gather.30.cloned.1.call-done = bf16[8192,2048]{1,0:T(8,128)(2,1)} async-done(((bf16[2048,2048]{1,0:T(8,128)(2,1)}), bf16[8192,2048]{1,0:T(8,128)(2,1)}) %all-gather.30.cloned.1.call-update) | async-done | bytes 33554448 | tf_op jit(solution)/shard_map/all_gather | solution.py:226
  1414.0 16.6 multiply_reduce_fusion.5
  1434.0 23.2 multiply_convert_fusion
  1457.2 16.9 fusion.107
  1474.1 21.0 multiply_reduce_fusion.1
  1516.8 80.1 %while.50 = (s32[]{:T(128)}, f32[256,16,128]{0,2,1:T(8,128)}, bf16[2048,2048]{0,1:T(8,128)(2,1)}, bf16[2048,2048]{0,1:T(8,128)(2,1)}, bf16[2048,2048]{0,1:T(8,12...) while((s32[]{:T(128)}, f32[256,16,128]{0,2,1:T(8,128)}, ...), condition=%wide.region_13.14_spmd.clone, body=%wide.region_12.13_spmd.clone.sunk | while | flops 2709129728 | bytes 99024728 | solution.py:305
  1598.9 16.4 convolution_convert_fusion.1
  1624.3 62.5 %reduce-scatter.10.cloned.1.call-done = bf16[256,2048]{0,1:T(8,128)(2,1)} async-done(((bf16[2048,2048]{0,1:T(8,128)(2,1)}), bf16[256,2048]{0,1:T(8,128)(2,1)}) %reduce-scatter.10.cloned.1.call-update) | async-done | bytes 1048592 | tf_op jit(solution)/shard_map/reduce_scatter | solution.py:312
  1693.9 83.6 %reduce-scatter.12.cloned.1.call-done = bf16[256,2048]{0,1:T(8,128)(2,1)} async-done(((bf16[2048,2048]{0,1:T(8,128)(2,1)}), bf16[256,2048]{0,1:T(8,128)(2,1)}) %reduce-scatter.12.cloned.1.call-update) | async-done | bytes 1048592 | tf_op jit(solution)/shard_map/reduce_scatter | solution.py:315
  1777.5 13.3 convert_bitcast_fusion
  1790.8 24.4 pad_maximum_fusion
  1816.4 29.1 convolution_convert_fusion
  1847.0 220.6 %reduce-scatter.18.cloned.1.call-done = bf16[2048,2048]{1,0:T(8,128)(2,1)} async-done(((bf16[8192,2048]{1,0:T(8,128)(2,1)}), bf16[2048,2048]{1,0:T(8,128)(2,1)}) %reduce-scatter.18.cloned.1.call-update) | async-done | bytes 8388624
  2067.6 291.9 %reduce-scatter.14.cloned.1.call-done = bf16[512,8192]{0,1:T(8,128)(2,1)} async-done(((bf16[2048,8192]{0,1:T(8,128)(2,1)}), bf16[512,8192]{0,1:T(8,128)(2,1)}) %reduce-scatter.14.cloned.1.call-update) | async-done | bytes 8388624 | tf_op jit(solution)/shard_map/reduce_scatter | solution.py:338
  2359.5 561.4 %reduce-scatter.16.cloned.1.call-done = bf16[512,16384]{1,0:T(8,128)(2,1)} async-done(((bf16[2048,16384]{1,0:T(8,128)(2,1)}), bf16[512,16384]{1,0:T(8,128)(2,1)}) %reduce-scatter.16.cloned.1.call-update) | async-done | bytes 16777232
  2924.8 39.9 %all-reduce.6 = (f32[4,2048]{1,0:T(4,128)S(1)}, f32[4]{0:T(128)S(1)}) all-reduce(f32[4,2048]{1,0:T(4,128)S(1)} %pad_maximum_fusion.3, f32[4]{0:T(128)S(1)} %pad_maximum_fusion.4), channel_id=1, replica_groups=mesh['replica'=8,'shard'=4] {'replica','shard'}, use_global_device_ids=true, to_apply=%region_28.29 | all-reduce | flops 8196 | bytes 65568 | tf_op jit(solution)/shard_map/psum | solution.py:362
  2967.1 7.1 fusion.108
  2974.2 36.2 all-gather.32.cloned.1.call-done
  3010.4 7.7 convolution_add_fusion.2
  3018.1 81.7 %all-gather.34.cloned.1.call-done = bf16[2048,2048]{1,0:T(8,128)(2,1)} async-done(((bf16[512,2048]{1,0:T(8,128)(2,1)}), bf16[2048,2048]{1,0:T(8,128)(2,1)}) %all-gather.34.cloned.1.call-update) | async-done | bytes 8388624 | tf_op jit(solution)/shard_map/all_gather | solution.py:329
  3099.8 8.4 fusion.65
  3108.1 645.1 %all-reduce.10.cloned.1.call-done = (bf16[512,8192]{0,1:T(8,128)(2,1)}, bf16[512,16384]{1,0:T(8,128)(2,1)}, bf16[2048,2048]{1,0:T(8,128)(2,1)}) async-done(((bf16[512,8192]{0,1:T(8,128)(2,1)}, bf16[512,16384]{1,0:T(8,128)(2,1)}, bf16[2048,2048]{1,0:T(8,128)(2,1)}), (bf16[512,8192]{0,1:T(8,128)(2,1)}, bf16[512,16384]{1,0:T(8,128)(2,1)}, bf16[2048,2048]{1,0:T(8,128)(2,1)})) %all-reduce.10.cloned.1.call-update) | async-done | bytes 33554448 | tf_op jit(solution)/shard_map/psum | solution.py:348
  3753.2 16.9 fusion.100
  3770.1 10.4 fusion.101
  3801.9 11.7 convert_element_type.211
  (376 shorter events, 245.5 us)
Async XLA Ops:
  7.2 165.3 %all-gather.16.cloned.1.call-start = ((), (), s32[]{:S(2)}) async-start(), calls=%async_computation.5 | async-start | bytes 20971520 | tf_op jit(solution)/shard_map/all_gather | solution.py:109
  12.0 160.5 %copy-start.17 = (bf16[1,256,2048]{2,1,0:T(8,128)(2,1)S(1)}, bf16[1,256,2048]{2,1,0:T(8,128)(2,1)}, u32[]{:S(2)}) copy-start(bf16[1,256,2048]{2,1,0:T(8,128)(2,1)} %param.21) | copy-start | bytes 3145732
  12.0 249.9 %all-gather.22.cloned.1.call-start = ((), (), s32[]{:S(2)}) async-start(), calls=%async_computation.8 | async-start | bytes 10485760 | tf_op jit(solution)/shard_map/all_gather | solution.py:107
  12.8 333.9 %all-gather.20.cloned.1.call-start = ((), (), s32[]{:S(2)}) async-start(), calls=%async_computation.7 | async-start | bytes 9437184 | tf_op jit(solution)/shard_map/all_gather | solution.py:153
  46.0 225.5 %copy-start.24 = (f32[256,64]{0,1:T(8,128)}, f32[256,64]{0,1:T(8,128)S(1)}, u32[]{:S(2)}) copy-start(f32[256,64]{0,1:T(8,128)S(1)} %get-tuple-element.949) | copy-start | bytes 196612
  46.0 225.5 %copy-start.26 = (f32[256,64]{0,1:T(8,128)}, f32[256,64]{0,1:T(8,128)S(1)}, u32[]{:S(2)}) copy-start(f32[256,64]{0,1:T(8,128)S(1)} %get-tuple-element.950) | copy-start | bytes 196612
  46.7 131.9 %copy-start.36 = (f32[1,2048]{1,0:T(1,128)}, f32[1,2048]{1,0:T(1,128)S(1)}, u32[]{:S(2)}) copy-start(f32[1,2048]{1,0:T(1,128)S(1)} %get-tuple-element.948) | copy-start | bytes 24580
  46.7 224.5 %copy-start.34 = (f32[1,2048]{1,0:T(1,128)}, f32[1,2048]{1,0:T(1,128)S(1)}, u32[]{:S(2)}) copy-start(f32[1,2048]{1,0:T(1,128)S(1)} %get-tuple-element.947) | copy-start | bytes 24580
  180.9 248.5 %all-gather.18.cloned.1.call-start = ((), (), s32[]{:S(2)}) async-start(), calls=%async_computation.6 | async-start | bytes 9437184 | tf_op jit(solution)/shard_map/all_gather | solution.py:154
  189.0 327.9 %all-gather.24.cloned.1.call-start = ((), (), s32[]{:S(2)}) async-start(), calls=%async_computation.9 | async-start | bytes 10485760 | tf_op jit(solution)/shard_map/all_gather | solution.py:115
  189.6 626.3 %all-gather.26.cloned.1.call-start = ((), (), s32[]{:S(2)}) async-start(), calls=%async_computation.10 | async-start | bytes 41943040 | tf_op jit(solution)/shard_map/all_gather | solution.py:206
  190.2 924.8 %all-gather.28.cloned.1.call-start = ((), (), s32[]{:S(2)}) async-start(), calls=%async_computation.11 | async-start | bytes 41943040 | tf_op jit(solution)/shard_map/all_gather | solution.py:207
  190.9 1223.1 %all-gather.30.cloned.1.call-start = ((), (), s32[]{:S(2)}) async-start(), calls=%async_computation.12 | async-start | bytes 41943040 | tf_op jit(solution)/shard_map/all_gather | solution.py:226
  191.7 1495.1 %reduce-scatter.10.cloned.1.call-start = ((), (), s32[]{:S(2)}) async-start(), calls=%async_computation.13 | async-start | bytes 9437184 | tf_op jit(solution)/shard_map/reduce_scatter | solution.py:312
  272.5 74.1 %copy-start.4 = (bf16[256,16,128]{0,2,1:T(8,128)(2,1)}, bf16[256,16,128]{0,2,1:T(8,128)(2,1)S(1)}, u32[]{:S(2)}) copy-start(bf16[256,16,128]{0,2,1:T(8,128)(2,1)S(1)} %maximum_convert_fusion) | copy-start | bytes 3145732
  472.1 51.0 %copy-start.1 = (bf16[256,2048]{1,0:T(8,128)(2,1)}, bf16[256,2048]{1,0:T(8,128)(2,1)S(1)}, u32[]{:S(2)}) copy-start(bf16[256,2048]{1,0:T(8,128)(2,1)S(1)} %get-tuple-element.1320) | copy-start | bytes 3145732
  472.1 51.0 %copy-start.30 = (bf16[2048]{0:T(1024)(128)(2,1)}, bf16[2048]{0:T(1024)(128)(2,1)S(1)}, u32[]{:S(2)}) copy-start(bf16[2048]{0:T(1024)(128)(2,1)S(1)} %get-tuple-element.1365) | copy-start | bytes 12292
  472.1 51.0 %copy-start.32 = (f32[256]{0:T(256)}, f32[256]{0:T(256)S(1)}, u32[]{:S(2)}) copy-start(f32[256]{0:T(256)S(1)} %get-tuple-element.1367) | copy-start | bytes 3076
  472.1 51.0 %copy-start.40 = (f32[16,256]{1,0:T(8,128)}, f32[16,256]{1,0:T(8,128)S(1)}, u32[]{:S(2)}) copy-start(f32[16,256]{1,0:T(8,128)S(1)} %get-tuple-element.1368) | copy-start | bytes 49156
  516.9 6.3 copy-start.18
  523.6 591.3 %copy-start.15 = (bf16[256,2048]{1,0:T(8,128)(2,1)}, bf16[256,2048]{1,0:T(8,128)(2,1)S(1)}, u32[]{:S(2)}) copy-start(bf16[256,2048]{1,0:T(8,128)(2,1)S(1)} %fusion.86) | copy-start | bytes 3145732
  1414.0 17.9 copy-start.22
  1414.0 17.9 copy-start.38
  1414.0 17.9 copy-start.49
  1434.0 23.2 copy-start.47
  1474.1 23.1 slice-start
  1474.1 23.1 slice-start.1
  1500.0 4.4 copy-start.13
  1512.4 4.5 copy-start.2
  1512.4 4.5 copy-start.31
  1512.4 4.5 copy-start.33
  1512.4 4.5 copy-start.41
  1562.2 3.0 copy-start.5
  1597.0 180.5 %reduce-scatter.12.cloned.1.call-start = ((), (), s32[]{:S(2)}) async-start(), calls=%async_computation.15 | async-start | bytes 9437184 | tf_op jit(solution)/shard_map/reduce_scatter | solution.py:315
  1597.6 470.0 %reduce-scatter.18.cloned.1.call-start = ((), (), s32[]{:S(2)}) async-start(), calls=%async_computation.19 | async-start | bytes 41943040
  1615.3 3.2 copy-start.10
  1615.3 744.1 %reduce-scatter.14.cloned.1.call-start = ((), (), s32[]{:S(2)}) async-start(), calls=%async_computation.17 | async-start | bytes 41943040 | tf_op jit(solution)/shard_map/reduce_scatter | solution.py:338
  1624.3 63.9 %copy-start.14 = (f32[256,16,128]{0,2,1:T(8,128)S(1)}, f32[256,16,128]{0,2,1:T(8,128)}, u32[]{:S(2)}) copy-start(f32[256,16,128]{0,2,1:T(8,128)} %broadcast_multiply_fusion) | copy-start | bytes 6291460
  1624.3 63.9 %copy-start.25 = (f32[256,64]{0,1:T(8,128)S(1)}, f32[256,64]{0,1:T(8,128)}, u32[]{:S(2)}) copy-start(f32[256,64]{0,1:T(8,128)} %copy-done.24) | copy-start | bytes 196612
  1624.3 63.9 %copy-start.27 = (f32[256,64]{0,1:T(8,128)S(1)}, f32[256,64]{0,1:T(8,128)}, u32[]{:S(2)}) copy-start(f32[256,64]{0,1:T(8,128)} %copy-done.26) | copy-start | bytes 196612
  1693.4 84.1 %copy-start.19 = (bf16[1,256,2048]{2,1,0:T(8,128)(2,1)S(1)}, bf16[1,256,2048]{2,1,0:T(8,128)(2,1)}, u32[]{:S(2)}) copy-start(bf16[1,256,2048]{2,1,0:T(8,128)(2,1)} %param.21) | copy-start | bytes 3145732
  1815.2 1105.6 %reduce-scatter.16.cloned.1.call-start = ((), (), s32[]{:S(2)}) async-start(), calls=%async_computation.18 | async-start | bytes 83886080
  1845.5 1164.9 %all-gather.32.cloned.1.call-start = ((), (), s32[]{:S(2)}) async-start(), calls=%async_computation.14 | async-start | bytes 10485760 | tf_op jit(solution)/shard_map/all_gather | solution.py:328
  1846.1 1253.7 %all-gather.34.cloned.1.call-start = ((), (), s32[]{:S(2)}) async-start(), calls=%async_computation.16 | async-start | bytes 10485760 | tf_op jit(solution)/shard_map/all_gather | solution.py:329
  1846.7 1906.5 %all-reduce.10.cloned.1.call-start = ((), (), s32[]{:S(2)}) async-start(), calls=%async_computation.20 | async-start | bytes 67108864 | tf_op jit(solution)/shard_map/psum | solution.py:348
  2920.8 4.0 copy-start.39
  2920.8 4.0 copy-start.46
  2974.2 125.5 %copy-start.28 = (bf16[256,2048]{0,1:T(8,128)(2,1)S(1)}, bf16[256,2048]{0,1:T(8,128)(2,1)}, u32[]{:S(2)}) copy-start(bf16[256,2048]{0,1:T(8,128)(2,1)} %reduce-scatter.12.cloned.1.call-done) | copy-start | bytes 3145732
  (40 other events, 66.4 us)
Sparse Core Ops, SparseCore 0:
  12.1 160.2 all-gather.15
  174.3 87.5 all-gather.21
  264.1 82.4 all-gather.19
  348.7 80.6 all-gather.17
  431.1 85.7 all-gather.23
  518.6 297.2 all-gather.25
  817.7 297.2 all-gather.27
  1116.8 297.2 all-gather.29
  1597.1 89.5 reduce-scatter.9
  1689.5 87.9 reduce-scatter.11
  1780.6 286.9 reduce-scatter.17
  2070.8 288.6 reduce-scatter.13
  2362.5 558.2 reduce-scatter.15
  2922.5 87.8 all-gather.31
  3012.1 87.6 all-gather.33
  3102.5 650.6 all-reduce.9
